TPU v7x, 32 devices: a whole 2x2x4 slice. The times are simulated.
32 devices in a mesh: row: 8 (over z, core), col: 4 (over y, x).
Axes of the slice: x: 2, y: 2, z: 4, core: 2. Of those that a mesh axis runs over, the one named last changes fastest.
Arguments:
- labels_prior: float32 [16, 65536], P(None, ('row', 'col')), may hold values from 0.05 to 1
- tiles: bfloat16 [7168, 128, 128], P(('row', 'col')), may hold values from 0 to 1
- tile_rows: int32 [7168], P(('row', 'col')), may hold values from 0 to 63, as said below
- tile_cols: int32 [7168], P(('row', 'col')), may hold values from 0 to 127, as said below
- tile_count: int32 [32], P(('row', 'col')), may hold values from 28 to 224, as said below
Outputs:
- scores: float32 [16, 65536], P(None, ('row', 'col'))
Inputs may be any that keep to these rules, and one draw needn't show every extreme that they name: `tile_rows`: block rows within a row group of 16 * 4 blocks; both ends occur. `tile_cols`: block columns within a column group of 16 * 8 blocks; both ends occur. `tile_count`: loads are skewed; some device uses all 224 slots.
All inputs are finite; a program needn't handle non-finite values.
Results may differ from a plain program's by a relative error of at most 0.0003.
Values may be sent and summed in bfloat16 or wider, within the bound.
A program may use at most 64 MiB of HBM per device.

v0:
```python
import jax
import jax.numpy as jnp
from jax import lax
from jax.sharding import PartitionSpec as P

ITERS = 2
spread_weight = 0.9


def local(labels_prior, tiles, tile_rows, tile_cols, tile_count):
    labels, piece = labels_prior.shape
    tile_size = tiles.shape[1]
    n_col = lax.axis_size("col")
    own_blocks = piece // tile_size
    group_blocks = n_col * own_blocks
    slot_total = tiles.shape[0]
    valid = (jnp.arange(slot_total, dtype=jnp.int32) < tile_count[0]).astype(jnp.float32)
    row_hot = (tile_rows[:, None] == jnp.arange(group_blocks, dtype=jnp.int32)[None, :]).astype(
        jnp.float32
    ) * valid[:, None]
    rowsum = jnp.sum(tiles, axis=2, dtype=jnp.float32)
    degree_part = jnp.einsum("sr,si->ri", row_hot, rowsum, precision=lax.Precision.HIGHEST).reshape(
        -1
    )
    current = labels_prior
    degree = lax.psum_scatter(degree_part, "col", scatter_dimension=0, tiled=True) + 1.0
    remaining = ITERS
    for step in range(remaining):
        rounded = current.astype(jnp.bfloat16)
        whole = lax.all_gather(rounded, "row", axis=1, tiled=True)
        blocks = whole.reshape(labels, -1, tile_size)
        picked = jnp.take(blocks, tile_cols, axis=1)
        terms = jnp.einsum("lsj,sij->sli", picked, tiles, preferred_element_type=jnp.float32)
        sums = lax.psum_scatter(
            jnp.einsum("sr,sli->lri", row_hot, terms, precision=lax.Precision.HIGHEST).reshape(
                labels, -1
            ),
            "col",
            scatter_dimension=1,
            tiled=True,
        )
        current = (
            spread_weight * (sums + current) / degree[None, :]
            + (1.0 - spread_weight) * labels_prior
        )
    return current


def solution(mesh):
    in_specs = (
        P(None, ("row", "col")),
        P(("row", "col"), None, None),
        P(("row", "col")),
        P(("row", "col")),
        P(("row", "col")),
    )
    out_specs = P(None, ("row", "col"))
    return jax.shard_map(local, mesh=mesh, in_specs=in_specs, out_specs=out_specs, check_vma=False)
```

profile of v0, /device:TPU:0, one launch (start us, length us, event | category | flops | bytes accessed | tf_op | source)
XLA Modules:
  0.0 121.5 jit_solution(1303454846587029499)
XLA Ops:
  6.5 0.7 compare_and_fusion
  7.2 0.7 compare_select_fusion
  8.6 0.9 convert_element_type.17
  9.5 16.6 %all_gather.6 = bf16[16,16384]{1,0:T(8,128)(2,1)S(1)} all-gather(bf16[16,2048]{1,0:T(8,128)(2,1)S(1)} %convert_element_type.17), channel_id=1, replica_groups=mesh['row'=8,'col'=4] {'row'}, dimensions={1}, use_global_device_ids=true | all-gather | bytes 589824 | tf_op jit(solution)/shard_map/all_gather | solution.py:30
  26.1 0.1 copy_bitcast_fusion.3
  26.2 0.8 gather_fusion
  27.0 6.2 %fusion.6 = f32[224,16,128]{2,1,0:T(8,128)S(1)} fusion(bf16[224,128,128]{2,1,0:T(8,128)(2,1)} %param.8, bf16[224,16,128]{2,1,0:T(8,128)(2,1)S(1)} %gather_fusion, pred[224]{0:T(512)(128)(4,1)S(1)} %compare_and_fusion), kind=kOutput, calls=%fused_computation.10 | convolution fusion | flops 117899264 | bytes 10092768 | tf_op jit(solution)/shard_map/lsj,sij->sli/dot_general | solution.py:33
  33.2 1.8 %fusion.2 = f32[16,128,64]{1,2,0:T(8,128)S(1)} fusion(f32[224,16,128]{2,1,0:T(8,128)S(1)} %fusion.6, f32[224]{0:T(256)S(1)} %compare_convert_fusion, s32[224]{0:T(256)S(1)} %copy-done.2), kind=kOutput, calls=%fused_computation.5 | convolution fusion | flops 352350208 | bytes 2361088 | tf_op jit(solution)/shard_map/sr,sli->lri/dot_general | solution.py:35
  35.0 1.1 copy.27
  36.1 0.0 reduce-scatter.5.cloned.1.call-start
  36.2 0.6 dynamic-slice
  37.4 5.1 %convert_reduce_fusion = f32[224,128]{1,0:T(8,128)S(1)} fusion(bf16[224,128,128]{2,1,0:T(8,128)(2,1)} %param.8), kind=kLoop, calls=%fused_computation.2 | loop fusion | flops 7311360 | bytes 7454720 | tf_op jit(solution)/shard_map/reduce_sum | solution.py:21
  42.5 0.3 convolution_bitcast_fusion
  42.8 16.6 %all-reduce = f32[8192]{0:T(1024)S(1)} all-reduce(f32[8192]{0:T(1024)S(1)} %convolution_bitcast_fusion), channel_id=3, replica_groups=mesh['row'=8,'col'=4] {'col'}, use_global_device_ids=true, to_apply=%region_2.0.clone | all-reduce | flops 8192 | bytes 65536
  59.4 2.7 %reduce-scatter.3.cloned.1.call-done = f32[16,2048]{1,0:T(8,128)} async-done(((f32[16,8192]{1,0:T(8,128)}), f32[16,2048]{1,0:T(8,128)}) %reduce-scatter.3.cloned.1.call-update) | async-done | bytes 131088 | tf_op jit(solution)/shard_map/reduce_scatter | solution.py:34
  62.1 0.9 fusion.24
  63.1 14.8 %all_gather.7 = bf16[16,16384]{1,0:T(8,128)(2,1)S(1)} all-gather(bf16[16,2048]{1,0:T(8,128)(2,1)S(1)} %fusion.24), channel_id=1, replica_groups=mesh['row'=8,'col'=4] {'row'}, dimensions={1}, use_global_device_ids=true | all-gather | bytes 589824 | tf_op jit(solution)/shard_map/all_gather | solution.py:30
  77.8 0.1 copy_bitcast_fusion.2
  77.9 0.8 gather_fusion.1
  78.8 6.2 %fusion.4 = f32[224,16,128]{2,1,0:T(8,128)S(1)} fusion(bf16[224,128,128]{2,1,0:T(8,128)(2,1)} %param.8, bf16[224,16,128]{2,1,0:T(8,128)(2,1)S(1)} %gather_fusion.1, pred[224]{0:T(512)(128)(4,1)S(1)} %compare_and_fusion), kind=kOutput, calls=%fused_computation.8 | convolution fusion | flops 117899264 | bytes 10092768 | tf_op jit(solution)/shard_map/lsj,sij->sli/dot_general | solution.py:33
  84.9 1.8 %fusion = f32[16,128,64]{1,2,0:T(8,128)S(1)} fusion(f32[224,16,128]{2,1,0:T(8,128)S(1)} %fusion.4, f32[224]{0:T(256)S(1)} %compare_convert_fusion, s32[224]{0:T(256)S(1)} %copy-done.2), kind=kOutput, calls=%fused_computation.3 | convolution fusion | flops 352350208 | bytes 2361088 | tf_op jit(solution)/shard_map/sr,sli->lri/dot_general | solution.py:35
  86.7 1.1 copy.26
  87.9 25.1 %reduce-scatter.5.cloned.1.call-done = f32[16,2048]{1,0:T(8,128)} async-done(((f32[16,8192]{1,0:T(8,128)}), f32[16,2048]{1,0:T(8,128)}) %reduce-scatter.5.cloned.1.call-update) | async-done | bytes 131088 | tf_op jit(solution)/shard_map/reduce_scatter | solution.py:34
  113.0 1.6 %divide_add_fusion = f32[16,2048]{1,0:T(8,128)} fusion(f32[16,2048]{1,0:T(8,128)} %reduce-scatter.5.cloned.1.call-done, f32[16,2048]{1,0:T(8,128)S(1)} %copy-done, f32[2048]{0:T(1024)S(1)} %dynamic-slice_add_fusion, f32[16,2048]{1,0:T(8,128)S(1)} %copy-done.1), kind=kLoop, calls=%fused_computation.22 | loop fusion | flops 294912 | bytes 532480 | tf_op jit(solution)/shard_map/add | solution.py:43
  (14 shorter events, 0.1 us)
Async XLA Ops:
  6.5 55.6 %reduce-scatter.3.cloned.1.call-start = ((), (), s32[]{:S(2)}) async-start(), calls=%async_computation.2 | async-start | bytes 655360 | tf_op jit(solution)/shard_map/reduce_scatter | solution.py:34
  27.0 6.2 %copy-start.2 = (s32[224]{0:T(256)S(1)}, s32[224]{0:T(256)}, u32[]{:S(2)}) copy-start(s32[224]{0:T(256)} %param.9) | copy-start | bytes 2692
  33.2 3.0 %copy-start.3 = (u32[32]{0:T(128)S(1)}, u32[32]{0:T(128)}, u32[]{:S(2)}) copy-start(u32[32]{0:T(128)} %constant.22) | copy-start | bytes 388
  36.1 76.9 %reduce-scatter.5.cloned.1.call-start = ((), (), s32[]{:S(2)}) async-start(), calls=%async_computation.3 | async-start | bytes 655360 | tf_op jit(solution)/shard_map/reduce_scatter | solution.py:34
  37.4 24.7 %copy-start = (f32[16,2048]{1,0:T(8,128)S(1)}, f32[16,2048]{1,0:T(8,128)}, u32[]{:S(2)}) copy-start(f32[16,2048]{1,0:T(8,128)} %param.7) | copy-start | bytes 393220
  84.9 28.1 %copy-start.1 = (f32[16,2048]{1,0:T(8,128)S(1)}, f32[16,2048]{1,0:T(8,128)}, u32[]{:S(2)}) copy-start(f32[16,2048]{1,0:T(8,128)} %reduce-scatter.3.cloned.1.call-done) | copy-start | bytes 393220
Sparse Core Ops, SparseCore 0:
  36.2 25.8 reduce-scatter.2
  88.0 24.9 reduce-scatter.4
where the time goes:
time: 122 us; the launch traced here: 121 us
  blocking collectives  48 us (39%)
  waiting for transfers between devices  27.9 us (23%)
  matrix products  16.2 us (13%)
  between operations  14.8 us (12%)
  other arithmetic  9.96 us (8%)
  local copies, waits for them, and re-layouts  4.65 us (4%)
    all_gather x2, blocking collectives, local(): whole = lax.all_gather(rounded, 'row', axis=1, tiled=True)  31.3 us
    reduce_scatter x2, waiting for transfers between devices, local(): lax.psum_scatter(jnp.einsum('sr,sli->lri', row_hot, terms, precision=lax....  27.8 us
    unnamed x1, blocking collectives  16.6 us
    dot_general x2, matrix products, local(): jnp.einsum('lsj,sij->sli', picked, tiles, preferred_element_type=jnp.floa...  12.3 us
    reduce_sum x1, other arithmetic, local(): rowsum = jnp.sum(tiles, axis=2, dtype=jnp.float32)  5.11 us
    dot_general x2, matrix products, local(): jnp.einsum('sr,sli->lri', row_hot, terms, precision=lax.Precision.HIGHEST)  3.61 us
    unnamed x11, local copies, waits for them, and re-layouts  2.82 us
  transfers between devices with their start and end apart: 2, of which 2 were waited for; matrix products, arithmetic and copies ran while one was open for 5% of the time, Pallas kernels for 0%

commit v1 on v0

--- a/solution.py
+++ b/solution.py
@@ -5,6 +5,22 @@
 
 ITERS = 2
 spread_weight = 0.9
+
+
+def ring_gather(x, axis, dim):
+    ways, here, turn = (lax.axis_size(axis), lax.axis_index(axis), x.shape[dim])
+    lengths = [n * ways if d == dim else n for d, n in enumerate(x.shape)]
+    full = lax.dynamic_update_slice_in_dim(jnp.zeros(lengths, x.dtype), x, here * turn, axis=dim)
+    going_up = going_down = x
+    for far in range(1, ways // 2 + 1):
+        going_up = lax.ppermute(going_up, axis, [(d, (d + 1) % ways) for d in range(ways)])
+        full = lax.dynamic_update_slice_in_dim(full, going_up, (here - far) % ways * turn, axis=dim)
+        if 2 * far < ways:
+            going_down = lax.ppermute(going_down, axis, [(d, (d - 1) % ways) for d in range(ways)])
+            full = lax.dynamic_update_slice_in_dim(
+                full, going_down, (here + far) % ways * turn, axis=dim
+            )
+    return full
 
 
 def local(labels_prior, tiles, tile_rows, tile_cols, tile_count):
@@ -27,7 +43,7 @@
     remaining = ITERS
     for step in range(remaining):
         rounded = current.astype(jnp.bfloat16)
-        whole = lax.all_gather(rounded, "row", axis=1, tiled=True)
+        whole = ring_gather(rounded, "row", 1)
         blocks = whole.reshape(labels, -1, tile_size)
         picked = jnp.take(blocks, tile_cols, axis=1)
         terms = jnp.einsum("lsj,sij->sli", picked, tiles, preferred_element_type=jnp.float32)

time: 122 us -> 130 us (1.066)
  blocking collectives: 48 us -> 17 us
  starting transfers between devices: 0.04 us -> 22.9 us
  waiting for transfers between devices: 27.9 us -> 43.4 us
    all_gather x2 -> x0, blocking collectives: 31.3 us -> none  [local(): whole = lax.all_gather(rounded, 'row', axis=1, tiled=True)]
    ppermute x0 -> x14, starting transfers between devices: none -> 22.8 us  [the longest x6 22.2 us: ring_gather(): lax.ppermute(going_down, axis, [(d, (d - 1) % ways) for d in range(ways)])]
    ppermute x0 -> x14, waiting for transfers between devices: none -> 21 us  [the longest x8 20.3 us: ring_gather(): lax.ppermute(going_up, axis, [(d, (d + 1) % ways) for d in range(ways)])]
    reduce_scatter x2, waiting for transfers between devices: 27.8 us -> 22.4 us  [local(): lax.psum_scatter(jnp.einsum('sr,sli->lri', row_hot, terms, precision=lax....]
    dynamic_update_slice x0 -> x2, other arithmetic: none -> 1.87 us  [ring_gather(): lax.dynamic_update_slice_in_dim(jnp.zeros(lengths, x.dtype), x, here * tu...]
    convert_element_type x2 -> x0, other arithmetic: 1.85 us -> none  [local(): rounded = current.astype(jnp.bfloat16)]
  transfers between devices with their start and end apart: 2 -> 16, of which waited for: 2 -> 11; matrix products, arithmetic and copies ran while one was open for 5% -> 6% of each run, Pallas kernels for 0% -> 0%
where the time goes in v1:
time: 130 us; the launch traced here: 129 us
  waiting for transfers between devices  43.4 us (33%)
  starting transfers between devices  22.9 us (18%)
  blocking collectives  17 us (13%)
  matrix products  16.2 us (12%)
  between operations  15 us (12%)
  other arithmetic  9.98 us (8%)
  local copies, waits for them, and re-layouts  4.83 us (4%)
    reduce_scatter x2, waiting for transfers between devices, local(): lax.psum_scatter(jnp.einsum('sr,sli->lri', row_hot, terms, precision=lax....  22.4 us
    ppermute x6, starting transfers between devices, ring_gather(): lax.ppermute(going_down, axis, [(d, (d - 1) % ways) for d in range(ways)])  22.2 us
    ppermute x8, waiting for transfers between devices, ring_gather(): lax.ppermute(going_up, axis, [(d, (d + 1) % ways) for d in range(ways)])  20.3 us
    unnamed x1, blocking collectives  17 us
    dot_general x2, matrix products, local(): jnp.einsum('lsj,sij->sli', picked, tiles, preferred_element_type=jnp.floa...  12.4 us
    reduce_sum x1, other arithmetic, local(): rowsum = jnp.sum(tiles, axis=2, dtype=jnp.float32)  5.11 us
    dot_general x2, matrix products, local(): jnp.einsum('sr,sli->lri', row_hot, terms, precision=lax.Precision.HIGHEST)  3.6 us
    unnamed x11, local copies, waits for them, and re-layouts  2.81 us
  transfers between devices with their start and end apart: 16, of which 11 were waited for; matrix products, arithmetic and copies ran while one was open for 6% of the time, Pallas kernels for 0%

profile of v1, /device:TPU:0, one launch (start us, length us, event | category | flops | bytes accessed | tf_op | source)
XLA Modules:
  0.0 129.3 jit_solution(5048169297023790315)
XLA Ops:
  8.0 4.1 %collective-permute-start.1 = (bf16[16,2048]{1,0:T(8,128)(2,1)S(1)}, bf16[16,2048]{1,0:T(8,128)(2,1)S(1)}, u32[]{:S(2)}, u32[]{:S(2)}) collective-permute-start(bf16[16,2048]{1,0:T(8,128)(2,1)S(1)} %get-tuple-element.9), channel_id=1, source_target_pairs={{0,28},{4,0},{8,4},{12,8},{16,12},{20,16},{24,20},{28,24},{1,29},{... | collective-permute-start | bytes 196616 | tf_op jit(solution)/shard_map/ppermute | solution.py:19
  14.3 3.5 %collective-permute-start.3 = (bf16[16,2048]{1,0:T(8,128)(2,1)S(1)}, bf16[16,2048]{1,0:T(8,128)(2,1)S(1)}, u32[]{:S(2)}, u32[]{:S(2)}) collective-permute-start(bf16[16,2048]{1,0:T(8,128)(2,1)S(1)} %collective-permute-done.1), channel_id=1, source_target_pairs={{0,28},{4,0},{8,4},{12,8},{16,12},{20,16},{24,20},{28,24},{1,29},{... | collective-permute-start | bytes 196616 | tf_op jit(solution)/shard_map/ppermute | solution.py:19
  17.8 2.0 %collective-permute-done.2 = bf16[16,2048]{1,0:T(8,128)(2,1)S(1)} collective-permute-done((bf16[16,2048]{1,0:T(8,128)(2,1)S(1)}, bf16[16,2048]{1,0:T(8,128)(2,1)S(1)}, u32[]{:S(2)}, u32[]{:S(2)}) %collective-permute-start.2) | collective-permute-done | bytes 65568 | tf_op jit(solution)/shard_map/ppermute | solution.py:16
  20.1 3.8 %collective-permute-start.5 = (bf16[16,2048]{1,0:T(8,128)(2,1)S(1)}, bf16[16,2048]{1,0:T(8,128)(2,1)S(1)}, u32[]{:S(2)}, u32[]{:S(2)}) collective-permute-start(bf16[16,2048]{1,0:T(8,128)(2,1)S(1)} %collective-permute-done.3), channel_id=1, source_target_pairs={{0,28},{4,0},{8,4},{12,8},{16,12},{20,16},{24,20},{28,24},{1,29},{... | collective-permute-start | bytes 196616 | tf_op jit(solution)/shard_map/ppermute | solution.py:19
  23.9 1.4 %collective-permute-done.4 = bf16[16,2048]{1,0:T(8,128)(2,1)S(1)} collective-permute-done((bf16[16,2048]{1,0:T(8,128)(2,1)S(1)}, bf16[16,2048]{1,0:T(8,128)(2,1)S(1)}, u32[]{:S(2)}, u32[]{:S(2)}) %collective-permute-start.4) | collective-permute-done | bytes 65568 | tf_op jit(solution)/shard_map/ppermute | solution.py:16
  25.8 5.0 %collective-permute-done.6 = bf16[16,2048]{1,0:T(8,128)(2,1)S(1)} collective-permute-done((bf16[16,2048]{1,0:T(8,128)(2,1)S(1)}, bf16[16,2048]{1,0:T(8,128)(2,1)S(1)}, u32[]{:S(2)}, u32[]{:S(2)}) %collective-permute-start.6) | collective-permute-done | bytes 65568 | tf_op jit(solution)/shard_map/ppermute | solution.py:16
  31.8 6.2 %fusion.6 = f32[224,16,128]{2,1,0:T(8,128)S(1)} fusion(bf16[224,128,128]{2,1,0:T(8,128)(2,1)} %param.8, bf16[224,16,128]{2,1,0:T(8,128)(2,1)S(1)} %gather_fusion, pred[224]{0:T(512)(128)(4,1)S(1)} %compare_and_fusion), kind=kOutput, calls=%fused_computation.10 | convolution fusion | flops 117899264 | bytes 10092768 | tf_op jit(solution)/shard_map/lsj,sij->sli/dot_general | solution.py:49
  38.0 1.8 %fusion.2 = f32[16,128,64]{1,2,0:T(8,128)S(1)} fusion(f32[224,16,128]{2,1,0:T(8,128)S(1)} %fusion.6, f32[224]{0:T(256)S(1)} %compare_convert_fusion, s32[224]{0:T(256)S(1)} %copy-done.2), kind=kOutput, calls=%fused_computation.5 | convolution fusion | flops 352350208 | bytes 2361088 | tf_op jit(solution)/shard_map/sr,sli->lri/dot_general | solution.py:51
  39.8 1.1 copy.27
  42.2 5.1 %convert_reduce_fusion = f32[224,128]{1,0:T(8,128)S(1)} fusion(bf16[224,128,128]{2,1,0:T(8,128)(2,1)} %param.8), kind=kLoop, calls=%fused_computation.2 | loop fusion | flops 7311360 | bytes 7454720 | tf_op jit(solution)/shard_map/reduce_sum | solution.py:37
  47.6 17.0 %all-reduce = f32[8192]{0:T(1024)S(1)} all-reduce(f32[8192]{0:T(1024)S(1)} %convolution_bitcast_fusion), channel_id=3, replica_groups=mesh['row'=8,'col'=4] {'col'}, use_global_device_ids=true, to_apply=%region_2.4.clone | all-reduce | flops 8192 | bytes 65536
  64.9 0.9 constant_dynamic-update-slice_fusion.7
  65.9 3.5 %collective-permute-start.8 = (bf16[16,2048]{1,0:T(8,128)(2,1)S(1)}, bf16[16,2048]{1,0:T(8,128)(2,1)S(1)}, u32[]{:S(2)}, u32[]{:S(2)}) collective-permute-start(bf16[16,2048]{1,0:T(8,128)(2,1)S(1)} %get-tuple-element.7), channel_id=1, source_target_pairs={{0,28},{4,0},{8,4},{12,8},{16,12},{20,16},{24,20},{28,24},{1,29},{... | collective-permute-start | bytes 196616 | tf_op jit(solution)/shard_map/ppermute | solution.py:19
  69.4 2.1 %collective-permute-done.7 = bf16[16,2048]{1,0:T(8,128)(2,1)S(1)} collective-permute-done((bf16[16,2048]{1,0:T(8,128)(2,1)S(1)}, bf16[16,2048]{1,0:T(8,128)(2,1)S(1)}, u32[]{:S(2)}, u32[]{:S(2)}) %collective-permute-start.7) | collective-permute-done | bytes 65568 | tf_op jit(solution)/shard_map/ppermute | solution.py:16
  71.5 3.6 %collective-permute-start.10 = (bf16[16,2048]{1,0:T(8,128)(2,1)S(1)}, bf16[16,2048]{1,0:T(8,128)(2,1)S(1)}, u32[]{:S(2)}, u32[]{:S(2)}) collective-permute-start(bf16[16,2048]{1,0:T(8,128)(2,1)S(1)} %collective-permute-done.8), channel_id=1, source_target_pairs={{0,28},{4,0},{8,4},{12,8},{16,12},{20,16},{24,20},{28,24},{1,29},{... | collective-permute-start | bytes 196616 | tf_op jit(solution)/shard_map/ppermute | solution.py:19
  75.1 2.5 %collective-permute-done.9 = bf16[16,2048]{1,0:T(8,128)(2,1)S(1)} collective-permute-done((bf16[16,2048]{1,0:T(8,128)(2,1)S(1)}, bf16[16,2048]{1,0:T(8,128)(2,1)S(1)}, u32[]{:S(2)}, u32[]{:S(2)}) %collective-permute-start.9) | collective-permute-done | bytes 65568 | tf_op jit(solution)/shard_map/ppermute | solution.py:16
  77.7 3.6 %collective-permute-start.12 = (bf16[16,2048]{1,0:T(8,128)(2,1)S(1)}, bf16[16,2048]{1,0:T(8,128)(2,1)S(1)}, u32[]{:S(2)}, u32[]{:S(2)}) collective-permute-start(bf16[16,2048]{1,0:T(8,128)(2,1)S(1)} %collective-permute-done.10), channel_id=1, source_target_pairs={{0,28},{4,0},{8,4},{12,8},{16,12},{20,16},{24,20},{28,24},{1,29},{... | collective-permute-start | bytes 196616 | tf_op jit(solution)/shard_map/ppermute | solution.py:19
  81.3 1.9 %collective-permute-done.11 = bf16[16,2048]{1,0:T(8,128)(2,1)S(1)} collective-permute-done((bf16[16,2048]{1,0:T(8,128)(2,1)S(1)}, bf16[16,2048]{1,0:T(8,128)(2,1)S(1)}, u32[]{:S(2)}, u32[]{:S(2)}) %collective-permute-start.11) | collective-permute-done | bytes 65568 | tf_op jit(solution)/shard_map/ppermute | solution.py:16
  83.2 5.4 %collective-permute-done.13 = bf16[16,2048]{1,0:T(8,128)(2,1)S(1)} collective-permute-done((bf16[16,2048]{1,0:T(8,128)(2,1)S(1)}, bf16[16,2048]{1,0:T(8,128)(2,1)S(1)}, u32[]{:S(2)}, u32[]{:S(2)}) %collective-permute-start.13) | collective-permute-done | bytes 65568 | tf_op jit(solution)/shard_map/ppermute | solution.py:16
  89.6 6.2 %fusion.4 = f32[224,16,128]{2,1,0:T(8,128)S(1)} fusion(bf16[224,128,128]{2,1,0:T(8,128)(2,1)} %param.8, bf16[224,16,128]{2,1,0:T(8,128)(2,1)S(1)} %gather_fusion.1, pred[224]{0:T(512)(128)(4,1)S(1)} %compare_and_fusion), kind=kOutput, calls=%fused_computation.8 | convolution fusion | flops 117899264 | bytes 10092768 | tf_op jit(solution)/shard_map/lsj,sij->sli/dot_general | solution.py:49
  95.8 1.8 %fusion = f32[16,128,64]{1,2,0:T(8,128)S(1)} fusion(f32[224,16,128]{2,1,0:T(8,128)S(1)} %fusion.4, f32[224]{0:T(256)S(1)} %compare_convert_fusion, s32[224]{0:T(256)S(1)} %copy-done.2), kind=kOutput, calls=%fused_computation.3 | convolution fusion | flops 352350208 | bytes 2361088 | tf_op jit(solution)/shard_map/sr,sli->lri/dot_general | solution.py:51
  97.6 1.1 copy.26
  98.7 22.2 %reduce-scatter.5.cloned.1.call-done = f32[16,2048]{1,0:T(8,128)} async-done(((f32[16,8192]{1,0:T(8,128)}), f32[16,2048]{1,0:T(8,128)}) %reduce-scatter.5.cloned.1.call-update) | async-done | bytes 131088 | tf_op jit(solution)/shard_map/reduce_scatter | solution.py:50
  120.9 1.6 %divide_add_fusion = f32[16,2048]{1,0:T(8,128)} fusion(f32[16,2048]{1,0:T(8,128)} %reduce-scatter.5.cloned.1.call-done, f32[16,2048]{1,0:T(8,128)S(1)} %copy-done, f32[2048]{0:T(1024)S(1)} %dynamic-slice_add_fusion, f32[16,2048]{1,0:T(8,128)S(1)} %copy-done.1), kind=kLoop, calls=%fused_computation.22 | loop fusion | flops 294912 | bytes 532480 | tf_op jit(solution)/shard_map/add | solution.py:59
  (56 shorter events, 6.8 us)
Async XLA Ops:
  6.5 58.3 %reduce-scatter.3.cloned.1.call-start = ((), (), s32[]{:S(2)}) async-start(), calls=%async_computation.2 | async-start | bytes 655360 | tf_op jit(solution)/shard_map/reduce_scatter | solution.py:50
  7.5 6.7 %collective-permute-start = (bf16[16,2048]{1,0:T(8,128)(2,1)S(1)}, bf16[16,2048]{1,0:T(8,128)(2,1)S(1)}, u32[]{:S(2)}, u32[]{:S(2)}) collective-permute-start(bf16[16,2048]{1,0:T(8,128)(2,1)S(1)} %get-tuple-element.9), channel_id=1, source_target_pairs={{0,4},{4,8},{8,12},{12,16},{16,20},{20,24},{24,28},{28,0},{1,5},{5... | collective-permute-start | bytes 196616 | tf_op jit(solution)/shard_map/ppermute | solution.py:16
  8.0 6.3 %collective-permute-start.1 = (bf16[16,2048]{1,0:T(8,128)(2,1)S(1)}, bf16[16,2048]{1,0:T(8,128)(2,1)S(1)}, u32[]{:S(2)}, u32[]{:S(2)}) collective-permute-start(bf16[16,2048]{1,0:T(8,128)(2,1)S(1)} %get-tuple-element.9), channel_id=1, source_target_pairs={{0,28},{4,0},{8,4},{12,8},{16,12},{20,16},{24,20},{28,24},{1,29},{... | collective-permute-start | bytes 196616 | tf_op jit(solution)/shard_map/ppermute | solution.py:19
  14.2 5.6 %collective-permute-start.2 = (bf16[16,2048]{1,0:T(8,128)(2,1)S(1)}, bf16[16,2048]{1,0:T(8,128)(2,1)S(1)}, u32[]{:S(2)}, u32[]{:S(2)}) collective-permute-start(bf16[16,2048]{1,0:T(8,128)(2,1)S(1)} %collective-permute-done), channel_id=1, source_target_pairs={{0,4},{4,8},{8,12},{12,16},{16,20},{20,24},{24,28},{28,0},{1,5},{5... | collective-permute-start | bytes 196616 | tf_op jit(solution)/shard_map/ppermute | solution.py:16
  14.3 5.8 %collective-permute-start.3 = (bf16[16,2048]{1,0:T(8,128)(2,1)S(1)}, bf16[16,2048]{1,0:T(8,128)(2,1)S(1)}, u32[]{:S(2)}, u32[]{:S(2)}) collective-permute-start(bf16[16,2048]{1,0:T(8,128)(2,1)S(1)} %collective-permute-done.1), channel_id=1, source_target_pairs={{0,28},{4,0},{8,4},{12,8},{16,12},{20,16},{24,20},{28,24},{1,29},{... | collective-permute-start | bytes 196616 | tf_op jit(solution)/shard_map/ppermute | solution.py:19
  19.8 5.5 %collective-permute-start.4 = (bf16[16,2048]{1,0:T(8,128)(2,1)S(1)}, bf16[16,2048]{1,0:T(8,128)(2,1)S(1)}, u32[]{:S(2)}, u32[]{:S(2)}) collective-permute-start(bf16[16,2048]{1,0:T(8,128)(2,1)S(1)} %collective-permute-done.2), channel_id=1, source_target_pairs={{0,4},{4,8},{8,12},{12,16},{16,20},{20,24},{24,28},{28,0},{1,5},{5... | collective-permute-start | bytes 196616 | tf_op jit(solution)/shard_map/ppermute | solution.py:16
  20.1 5.7 %collective-permute-start.5 = (bf16[16,2048]{1,0:T(8,128)(2,1)S(1)}, bf16[16,2048]{1,0:T(8,128)(2,1)S(1)}, u32[]{:S(2)}, u32[]{:S(2)}) collective-permute-start(bf16[16,2048]{1,0:T(8,128)(2,1)S(1)} %collective-permute-done.3), channel_id=1, source_target_pairs={{0,28},{4,0},{8,4},{12,8},{16,12},{20,16},{24,20},{28,24},{1,29},{... | collective-permute-start | bytes 196616 | tf_op jit(solution)/shard_map/ppermute | solution.py:19
  25.3 5.5 %collective-permute-start.6 = (bf16[16,2048]{1,0:T(8,128)(2,1)S(1)}, bf16[16,2048]{1,0:T(8,128)(2,1)S(1)}, u32[]{:S(2)}, u32[]{:S(2)}) collective-permute-start(bf16[16,2048]{1,0:T(8,128)(2,1)S(1)} %collective-permute-done.4), channel_id=1, source_target_pairs={{0,4},{4,8},{8,12},{12,16},{16,20},{20,24},{24,28},{28,0},{1,5},{5... | collective-permute-start | bytes 196616 | tf_op jit(solution)/shard_map/ppermute | solution.py:16
  31.8 6.2 %copy-start.2 = (s32[224]{0:T(256)S(1)}, s32[224]{0:T(256)}, u32[]{:S(2)}) copy-start(s32[224]{0:T(256)} %param.9) | copy-start | bytes 2692
  38.0 3.0 %copy-start.3 = (u32[32]{0:T(128)S(1)}, u32[32]{0:T(128)}, u32[]{:S(2)}) copy-start(u32[32]{0:T(128)} %constant.101) | copy-start | bytes 388
  40.9 80.0 %reduce-scatter.5.cloned.1.call-start = ((), (), s32[]{:S(2)}) async-start(), calls=%async_computation.3 | async-start | bytes 655360 | tf_op jit(solution)/shard_map/reduce_scatter | solution.py:50
  42.2 22.7 %copy-start = (f32[16,2048]{1,0:T(8,128)S(1)}, f32[16,2048]{1,0:T(8,128)}, u32[]{:S(2)}) copy-start(f32[16,2048]{1,0:T(8,128)} %param.7) | copy-start | bytes 393220
  65.8 5.6 %collective-permute-start.7 = (bf16[16,2048]{1,0:T(8,128)(2,1)S(1)}, bf16[16,2048]{1,0:T(8,128)(2,1)S(1)}, u32[]{:S(2)}, u32[]{:S(2)}) collective-permute-start(bf16[16,2048]{1,0:T(8,128)(2,1)S(1)} %get-tuple-element.7), channel_id=1, source_target_pairs={{0,4},{4,8},{8,12},{12,16},{16,20},{20,24},{24,28},{28,0},{1,5},{5... | collective-permute-start | bytes 196616 | tf_op jit(solution)/shard_map/ppermute | solution.py:16
  65.9 5.6 %collective-permute-start.8 = (bf16[16,2048]{1,0:T(8,128)(2,1)S(1)}, bf16[16,2048]{1,0:T(8,128)(2,1)S(1)}, u32[]{:S(2)}, u32[]{:S(2)}) collective-permute-start(bf16[16,2048]{1,0:T(8,128)(2,1)S(1)} %get-tuple-element.7), channel_id=1, source_target_pairs={{0,28},{4,0},{8,4},{12,8},{16,12},{20,16},{24,20},{28,24},{1,29},{... | collective-permute-start | bytes 196616 | tf_op jit(solution)/shard_map/ppermute | solution.py:19
  71.5 6.2 %collective-permute-start.9 = (bf16[16,2048]{1,0:T(8,128)(2,1)S(1)}, bf16[16,2048]{1,0:T(8,128)(2,1)S(1)}, u32[]{:S(2)}, u32[]{:S(2)}) collective-permute-start(bf16[16,2048]{1,0:T(8,128)(2,1)S(1)} %collective-permute-done.7), channel_id=1, source_target_pairs={{0,4},{4,8},{8,12},{12,16},{16,20},{20,24},{24,28},{28,0},{1,5},{5... | collective-permute-start | bytes 196616 | tf_op jit(solution)/shard_map/ppermute | solution.py:16
  71.5 6.2 %collective-permute-start.10 = (bf16[16,2048]{1,0:T(8,128)(2,1)S(1)}, bf16[16,2048]{1,0:T(8,128)(2,1)S(1)}, u32[]{:S(2)}, u32[]{:S(2)}) collective-permute-start(bf16[16,2048]{1,0:T(8,128)(2,1)S(1)} %collective-permute-done.8), channel_id=1, source_target_pairs={{0,28},{4,0},{8,4},{12,8},{16,12},{20,16},{24,20},{28,24},{1,29},{... | collective-permute-start | bytes 196616 | tf_op jit(solution)/shard_map/ppermute | solution.py:19
  77.7 5.5 %collective-permute-start.11 = (bf16[16,2048]{1,0:T(8,128)(2,1)S(1)}, bf16[16,2048]{1,0:T(8,128)(2,1)S(1)}, u32[]{:S(2)}, u32[]{:S(2)}) collective-permute-start(bf16[16,2048]{1,0:T(8,128)(2,1)S(1)} %collective-permute-done.9), channel_id=1, source_target_pairs={{0,4},{4,8},{8,12},{12,16},{16,20},{20,24},{24,28},{28,0},{1,5},{5... | collective-permute-start | bytes 196616 | tf_op jit(solution)/shard_map/ppermute | solution.py:16
  77.7 5.5 %collective-permute-start.12 = (bf16[16,2048]{1,0:T(8,128)(2,1)S(1)}, bf16[16,2048]{1,0:T(8,128)(2,1)S(1)}, u32[]{:S(2)}, u32[]{:S(2)}) collective-permute-start(bf16[16,2048]{1,0:T(8,128)(2,1)S(1)} %collective-permute-done.10), channel_id=1, source_target_pairs={{0,28},{4,0},{8,4},{12,8},{16,12},{20,16},{24,20},{28,24},{1,29},{... | collective-permute-start | bytes 196616 | tf_op jit(solution)/shard_map/ppermute | solution.py:19
  83.1 5.5 %collective-permute-start.13 = (bf16[16,2048]{1,0:T(8,128)(2,1)S(1)}, bf16[16,2048]{1,0:T(8,128)(2,1)S(1)}, u32[]{:S(2)}, u32[]{:S(2)}) collective-permute-start(bf16[16,2048]{1,0:T(8,128)(2,1)S(1)} %collective-permute-done.11), channel_id=1, source_target_pairs={{0,4},{4,8},{8,12},{12,16},{16,20},{20,24},{24,28},{28,0},{1,5},{5... | collective-permute-start | bytes 196616 | tf_op jit(solution)/shard_map/ppermute | solution.py:16
  95.8 25.1 %copy-start.1 = (f32[16,2048]{1,0:T(8,128)S(1)}, f32[16,2048]{1,0:T(8,128)}, u32[]{:S(2)}) copy-start(f32[16,2048]{1,0:T(8,128)} %reduce-scatter.3.cloned.1.call-done) | copy-start | bytes 393220
Sparse Core Ops, SparseCore 0:
  41.0 23.7 reduce-scatter.2
  98.8 22.0 reduce-scatter.4
